TPU v7x, 32 devices: a whole 2x2x4 slice. The times are simulated.
32 devices in a mesh: dp: 8 (over z, x), fsdp: 4 (over y, core).
Axes of the slice: x: 2, y: 2, z: 4, core: 2. Of those that a mesh axis runs over, the one named last changes fastest.
Arguments:
- tokens: bfloat16 [2, 16, 1024, 768], P(None, 'dp', 'fsdp'), may hold values from -6 to 6
- cotangent: bfloat16 [2, 16, 1024, 768], P(None, 'dp', 'fsdp'), may hold values from -6 to 6
- lengths: int32 [2, 16], P(None, 'dp'), may hold values from 256 to 1024, as said below
- inward_weight: float32 [768, 2304], P('fsdp'), may hold values from -0.21875 to 0.21875
- outward_weight: float32 [768, 768], P('fsdp'), may hold values from -6 to 6
- expand_weight: float32 [768, 2304], P('fsdp'), may hold values from -0.21875 to 0.21875
- shrink_weight: float32 [1152, 768], P('fsdp'), may hold values from -0.1875 to 0.1875
- gain_weight: float32 [2, 768], P(None, 'fsdp'), may hold values from 0.5 to 1.5
- inward_first: float32 [768, 2304], P('fsdp'), may hold values from -2048 to 2048
- outward_first: float32 [768, 768], P('fsdp'), may hold values from -64 to 64
- expand_first: float32 [768, 2304], P('fsdp'), may hold values from -512 to 512
- shrink_first: float32 [1152, 768], P('fsdp'), may hold values from -512 to 512
- gain_first: float32 [2, 768], P(None, 'fsdp'), may hold values from -2048 to 2048
- inward_second: float32 [768, 2304], P('fsdp'), may hold values from 104857.6 to 419430.4
- outward_second: float32 [768, 768], P('fsdp'), may hold values from 131.072 to 524.288
- expand_second: float32 [768, 2304], P('fsdp'), may hold values from 6553.6 to 26214.4
- shrink_second: float32 [1152, 768], P('fsdp'), may hold values from 9502.72 to 38010.88
- gain_second: float32 [2, 768], P(None, 'fsdp'), may hold values from 104857.6 to 419430.4
Outputs:
- block_out: bfloat16 [2, 16, 1024, 768], P(None, 'dp', 'fsdp')
- input_grad: float32 [2, 16, 1024, 768], P(None, 'dp', 'fsdp')
- inward_renewed: float32 [768, 2304], P('fsdp')
- inward_momentum: float32 [768, 2304], P('fsdp')
- inward_variance: float32 [768, 2304], P('fsdp')
- outward_renewed: float32 [768, 768], P('fsdp')
- outward_momentum: float32 [768, 768], P('fsdp')
- outward_variance: float32 [768, 768], P('fsdp')
- expand_renewed: float32 [768, 2304], P('fsdp')
- expand_momentum: float32 [768, 2304], P('fsdp')
- expand_variance: float32 [768, 2304], P('fsdp')
- shrink_renewed: float32 [1152, 768], P('fsdp')
- shrink_momentum: float32 [1152, 768], P('fsdp')
- shrink_variance: float32 [1152, 768], P('fsdp')
- gain_renewed: float32 [2, 768], P(None, 'fsdp')
- gain_momentum: float32 [2, 768], P(None, 'fsdp')
- gain_variance: float32 [2, 768], P(None, 'fsdp')
Inputs may be any that keep to these rules, and one draw needn't show every extreme that they name: `lengths`: in each micro-batch, among the 2 sequences of each dp index, one has length 1024.
All inputs are finite; a program needn't handle non-finite values.
Results may differ from a plain program's by a relative error of at most 0.014.
Values may be sent and summed in bfloat16 or wider, within the bound.
No kernel may reach another device: no remote copies, remote signals or barrier semaphores. Data moves between devices by JAX's collectives and lax.ppermute only.
A program may use at most 256 MiB of HBM per device.

v0:
```python
import jax
import jax.numpy as jnp
from jax import lax
from jax.sharding import PartitionSpec as P

FF = 1152
HEADS = 12
HDIM = 64
STEP = 10
rope_base = 160000.0
norm_eps = 1e-05
adam_beta = 0.5
adam_eps = 1e-08
weight_decay = 0.01
rates = (0.07, 2.0, 0.07, 0.06, 0.2)
masked_score = -1e30


def tables(positions):
    half_dim = HDIM // 2
    exponent = jnp.arange(half_dim, dtype=jnp.float32) * (2.0 / HDIM)
    inverse = jnp.power(jnp.float32(rope_base), -exponent)
    angles = positions.astype(jnp.float32)[:, None] * inverse[None, :]
    return (jnp.cos(angles), jnp.sin(angles))


def rotate(values, cosine, sine_table):
    half_dim = values.shape[-1] // 2
    former = values[..., :half_dim]
    latter = values[..., half_dim:]
    cos_wide = cosine[:, None, :]
    sin_wide = sine_table[:, None, :]
    return jnp.concatenate(
        [former * cos_wide - latter * sin_wide, latter * cos_wide + former * sin_wide], axis=-1
    )


def normalize(values, gain_row):
    center = values - jnp.mean(values, axis=-1, keepdims=True)
    spread = jnp.mean(center * center, axis=-1, keepdims=True)
    return center * lax.rsqrt(spread + norm_eps) * gain_row


def geglu(joined_heads):
    gate_part = joined_heads[..., :FF]
    upward = joined_heads[..., FF:]
    return 0.5 * gate_part * (1.0 + lax.erf(gate_part * 0.7071067811865476)) * upward


def attention_scores(queries, keys_all, live_keys, score_scale):
    product = (
        jnp.einsum("sqhd,skhd->shqk", queries, keys_all, preferred_element_type=jnp.float32)
        * score_scale
    )
    return jnp.where(live_keys[:, None, None, :], product, masked_score)


def adam_update(master, gradient, moment_one, moment_two, step_rate, decay_rate):
    first_new = adam_beta * moment_one + (1.0 - adam_beta) * gradient
    second_new = adam_beta * moment_two + (1.0 - adam_beta) * gradient * gradient
    correction = 1.0 - adam_beta**STEP
    direction = first_new / correction / (jnp.sqrt(second_new / correction) + adam_eps)
    renewed = master - step_rate * (direction + decay_rate * master)
    return (renewed, first_new, second_new)


def local(
    tokens,
    cotangent,
    lengths,
    inward_weight,
    outward_weight,
    expand_weight,
    shrink_weight,
    gain_weight,
    inward_first,
    outward_first,
    expand_first,
    shrink_first,
    gain_first,
    inward_second,
    outward_second,
    expand_second,
    shrink_second,
    gain_second,
):
    micro_count, group_size, local_len, model_width = tokens.shape
    seq_total = local_len * lax.axis_size("fsdp")
    row_count = group_size * local_len
    score_scale = HDIM ** (-0.5)
    positions = lax.axis_index("fsdp") * local_len + jnp.arange(local_len, dtype=jnp.int32)
    cosine, sine_table = tables(positions)
    key_positions = jnp.arange(seq_total, dtype=jnp.int32)
    inward_copy = inward_weight.astype(jnp.bfloat16)
    outward_copy = outward_weight.astype(jnp.bfloat16)
    expand_copy = expand_weight.astype(jnp.bfloat16)
    shrink_copy = shrink_weight.astype(jnp.bfloat16)
    gain_copy = gain_weight.astype(jnp.bfloat16)
    accum = (
        jnp.zeros((model_width, 3 * model_width), jnp.float32),
        jnp.zeros((model_width, model_width), jnp.float32),
        jnp.zeros((model_width, 2 * FF), jnp.float32),
        jnp.zeros((FF, model_width), jnp.float32),
        jnp.zeros((2, model_width), jnp.float32),
    )

    def micro_step(accum, item):
        input_tokens, incoming, limits = item
        gathered = (
            lax.all_gather(inward_copy, "fsdp", axis=0, tiled=True),
            lax.all_gather(outward_copy, "fsdp", axis=0, tiled=True),
            lax.all_gather(expand_copy, "fsdp", axis=0, tiled=True),
            lax.all_gather(shrink_copy, "fsdp", axis=0, tiled=True),
            lax.all_gather(gain_copy, "fsdp", axis=1, tiled=True),
        )
        inward_matrix, outward_matrix, expand_matrix, shrink_matrix, gain_full = gathered
        gain_rows = gain_full.astype(jnp.float32)
        live_keys = key_positions[None, :] < limits[:, None]
        live_rows = (positions[None, :] < limits[:, None]).astype(jnp.float32).reshape(row_count, 1)
        flat_in = input_tokens.astype(jnp.float32).reshape(row_count, model_width)
        hidden_first_norm = normalize(flat_in, gain_rows[0]).astype(jnp.bfloat16)
        joined_heads = jnp.dot(
            hidden_first_norm, inward_matrix, preferred_element_type=jnp.float32
        ).reshape(group_size, local_len, 3, HEADS, HDIM)
        queries = rotate(joined_heads[:, :, 0], cosine, sine_table).astype(jnp.bfloat16)
        keys_local = rotate(joined_heads[:, :, 1], cosine, sine_table).astype(jnp.bfloat16)
        values_local = joined_heads[:, :, 2].astype(jnp.bfloat16)
        keys_all, values_all = (
            lax.all_gather(keys_local, "fsdp", axis=1, tiled=True),
            lax.all_gather(values_local, "fsdp", axis=1, tiled=True),
        )
        scores = attention_scores(queries, keys_all, live_keys, score_scale)
        row_peak = jnp.max(scores, axis=-1, keepdims=True)
        exp_terms = jnp.exp(scores - row_peak)
        totals = jnp.sum(exp_terms, axis=-1, keepdims=True)
        attention_low = (exp_terms / totals).astype(jnp.bfloat16)
        log_total = row_peak + jnp.log(totals)
        mixed_tokens = jnp.einsum(
            "shqk,skhd->sqhd", attention_low, values_all, preferred_element_type=jnp.float32
        )
        mixed_tokens = mixed_tokens.astype(jnp.bfloat16).reshape(row_count, model_width)
        middle_state = flat_in + jnp.dot(
            mixed_tokens, outward_matrix, preferred_element_type=jnp.float32
        )
        hidden_second_norm = normalize(middle_state, gain_rows[1]).astype(jnp.bfloat16)
        expanded_rows = jnp.dot(
            hidden_second_norm, expand_matrix, preferred_element_type=jnp.float32
        )
        hidden_state = geglu(expanded_rows).astype(jnp.bfloat16)
        layer_result = (
            middle_state + jnp.dot(hidden_state, shrink_matrix, preferred_element_type=jnp.float32)
        ) * live_rows
        block_rows = layer_result.astype(jnp.bfloat16).reshape(group_size, local_len, model_width)
        gathered_back = (
            lax.all_gather(inward_copy, "fsdp", axis=0, tiled=True),
            lax.all_gather(outward_copy, "fsdp", axis=0, tiled=True),
            lax.all_gather(expand_copy, "fsdp", axis=0, tiled=True),
            lax.all_gather(shrink_copy, "fsdp", axis=0, tiled=True),
            lax.all_gather(gain_copy, "fsdp", axis=1, tiled=True),
        )
        inward_back, outward_back, expand_back, shrink_back, gain_back = gathered_back
        gain_rows_back = gain_back.astype(jnp.float32)
        grad_out = incoming.astype(jnp.float32).reshape(row_count, model_width) * live_rows
        branch_low = grad_out.astype(jnp.bfloat16)
        shrink_grad = jnp.einsum(
            "rf,rd->fd", hidden_state, branch_low, preferred_element_type=jnp.float32
        )
        hidden_grad = jnp.einsum(
            "rd,fd->rf", branch_low, shrink_back, preferred_element_type=jnp.float32
        )
        unused, geglu_back = jax.vjp(geglu, expanded_rows)
        expanded_grad = geglu_back(hidden_grad)[0].astype(jnp.bfloat16)
        expand_grad = jnp.einsum(
            "rd,re->de", hidden_second_norm, expanded_grad, preferred_element_type=jnp.float32
        )
        h_two_grad = jnp.einsum(
            "re,de->rd", expanded_grad, expand_back, preferred_element_type=jnp.float32
        )
        unused, second_back = jax.vjp(normalize, middle_state, gain_rows_back[1])
        middle_part, gain_two_grad = second_back(h_two_grad)
        middle_grad = grad_out + middle_part
        mixer_low = middle_grad.astype(jnp.bfloat16)
        outward_grad = jnp.einsum(
            "rd,re->de", mixed_tokens, mixer_low, preferred_element_type=jnp.float32
        )
        mixed_grad = jnp.einsum(
            "re,de->rd", mixer_low, outward_back, preferred_element_type=jnp.float32
        )
        mixed_grad = mixed_grad.astype(jnp.bfloat16).reshape(group_size, local_len, HEADS, HDIM)
        scores_again = attention_scores(queries, keys_all, live_keys, score_scale)
        attention = jnp.exp(scores_again - log_total)
        attention_again = attention.astype(jnp.bfloat16)
        attention_grad = jnp.einsum(
            "sqhd,skhd->shqk", mixed_grad, values_all, preferred_element_type=jnp.float32
        )
        row_inner = jnp.sum(attention * attention_grad, axis=-1, keepdims=True)
        score_grad = (attention * (attention_grad - row_inner)).astype(jnp.bfloat16)
        query_grad = (
            jnp.einsum("shqk,skhd->sqhd", score_grad, keys_all, preferred_element_type=jnp.float32)
            * score_scale
        )
        key_part = (
            jnp.einsum("shqk,sqhd->skhd", score_grad, queries, preferred_element_type=jnp.float32)
            * score_scale
        )
        value_part = jnp.einsum(
            "shqk,sqhd->skhd", attention_again, mixed_grad, preferred_element_type=jnp.float32
        )
        key_grad, value_grad = (
            lax.psum_scatter(
                key_part.astype(jnp.bfloat16), "fsdp", scatter_dimension=1, tiled=True
            ).astype(jnp.float32),
            lax.psum_scatter(
                value_part.astype(jnp.bfloat16), "fsdp", scatter_dimension=1, tiled=True
            ).astype(jnp.float32),
        )
        joined_grad = jnp.stack(
            [
                rotate(query_grad, cosine, -sine_table),
                rotate(key_grad, cosine, -sine_table),
                value_grad,
            ],
            axis=2,
        )
        joined_grad = joined_grad.reshape(row_count, 3 * model_width).astype(jnp.bfloat16)
        inward_grad = jnp.einsum(
            "rd,re->de", hidden_first_norm, joined_grad, preferred_element_type=jnp.float32
        )
        h_one_grad = jnp.einsum(
            "re,de->rd", joined_grad, inward_back, preferred_element_type=jnp.float32
        )
        unused, first_back = jax.vjp(normalize, flat_in, gain_rows_back[0])
        input_part, gain_one_grad = first_back(h_one_grad)
        input_rows = (middle_grad + input_part).reshape(group_size, local_len, model_width)
        gain_grad = jnp.stack([gain_one_grad, gain_two_grad])
        accum = jax.tree.map(
            jnp.add, accum, (inward_grad, outward_grad, expand_grad, shrink_grad, gain_grad)
        )
        return (accum, (block_rows, input_rows))

    accum, outputs = lax.scan(micro_step, accum, (tokens, cotangent, lengths))
    block_out, input_grad = outputs
    shards = (
        lax.psum_scatter(
            accum[0].astype(jnp.bfloat16), "fsdp", scatter_dimension=0, tiled=True
        ).astype(jnp.float32),
        lax.psum_scatter(
            accum[1].astype(jnp.bfloat16), "fsdp", scatter_dimension=0, tiled=True
        ).astype(jnp.float32),
        lax.psum_scatter(
            accum[2].astype(jnp.bfloat16), "fsdp", scatter_dimension=0, tiled=True
        ).astype(jnp.float32),
        lax.psum_scatter(
            accum[3].astype(jnp.bfloat16), "fsdp", scatter_dimension=0, tiled=True
        ).astype(jnp.float32),
        lax.psum_scatter(
            accum[4].astype(jnp.bfloat16), "fsdp", scatter_dimension=1, tiled=True
        ).astype(jnp.float32),
    )
    shards = lax.psum((shards[0], shards[1], shards[2], shards[3], shards[4]), "dp")
    inward_new = adam_update(
        inward_weight, shards[0], inward_first, inward_second, rates[0], weight_decay
    )
    outward_new = adam_update(
        outward_weight, shards[1], outward_first, outward_second, rates[1], weight_decay
    )
    expand_new = adam_update(
        expand_weight, shards[2], expand_first, expand_second, rates[2], weight_decay
    )
    shrink_new = adam_update(
        shrink_weight, shards[3], shrink_first, shrink_second, rates[3], weight_decay
    )
    gain_new = adam_update(gain_weight, shards[4], gain_first, gain_second, rates[4], 0.0)
    return (
        block_out,
        input_grad,
        inward_new[0],
        inward_new[1],
        inward_new[2],
        outward_new[0],
        outward_new[1],
        outward_new[2],
        expand_new[0],
        expand_new[1],
        expand_new[2],
        shrink_new[0],
        shrink_new[1],
        shrink_new[2],
        gain_new[0],
        gain_new[1],
        gain_new[2],
    )


def solution(mesh):
    in_specs = (
        P(None, "dp", "fsdp", None),
        P(None, "dp", "fsdp", None),
        P(None, "dp"),
        P("fsdp", None),
        P("fsdp", None),
        P("fsdp", None),
        P("fsdp", None),
        P(None, "fsdp"),
        P("fsdp", None),
        P("fsdp", None),
        P("fsdp", None),
        P("fsdp", None),
        P(None, "fsdp"),
        P("fsdp", None),
        P("fsdp", None),
        P("fsdp", None),
        P("fsdp", None),
        P(None, "fsdp"),
    )
    out_specs = (
        P(None, "dp", "fsdp", None),
        P(None, "dp", "fsdp", None),
        P("fsdp", None),
        P("fsdp", None),
        P("fsdp", None),
        P("fsdp", None),
        P("fsdp", None),
        P("fsdp", None),
        P("fsdp", None),
        P("fsdp", None),
        P("fsdp", None),
        P("fsdp", None),
        P("fsdp", None),
        P("fsdp", None),
        P(None, "fsdp"),
        P(None, "fsdp"),
        P(None, "fsdp"),
    )
    return jax.shard_map(local, mesh=mesh, in_specs=in_specs, out_specs=out_specs, check_vma=False)
```

profile of v0, /device:TPU:0, one launch (start us, length us, event | category | flops | bytes accessed | tf_op | source)
XLA Modules:
  0.0 1104.0 jit_solution(12216921466018292153)
XLA Ops:
  14.0 698.6 %while.26 = (s32[]{:T(128)}, f32[768,2304]{1,0:T(8,128)}, f32[768,768]{1,0:T(8,128)}, f32[768,2304]{1,0:T(8,128)}, f32[1152,768]{1,0:T(8,128)}, /*index=5*/f32[2...) while((s32[]{:T(128)}, f32[768,2304]{1,0:T(8,128)}, ...), condition=%wide.region_16.17_spmd.clone.clone.clone, body=%wide.region_0.16_spmd.clone.clone.clone.sunk | while | flops 20481859584 | bytes 894956672 | solution.py:241
  15.0 6.0 all-gather.10
  23.4 27.1 %all-gather.19.cloned.1.call-done = bf16[768,2304]{1,0:T(8,128)(2,1)} async-done(((bf16[192,2304]{1,0:T(8,128)(2,1)}), bf16[768,2304]{1,0:T(8,128)(2,1)}) %all-gather.19.cloned.1.call-update) | async-done | bytes 3538960 | tf_op jit(solution)/shard_map/while/body/eval_jaxpr/all_gather | solution.py:110
  50.5 5.8 copy.94
  73.4 19.9 %all-gather.21.cloned.1.call-done = bf16[2,1024,12,64]{1,3,2,0:T(8,128)(2,1)} async-done(((bf16[2,256,12,64]{1,3,2,0:T(8,128)(2,1)}), bf16[2,1024,12,64]{1,3,2,0:T(8,128)(2,1)}) %all-gather.21.cloned.1.call-update) | async-done | bytes 3145744 | tf_op jit(solution)/shard_map/while/body/eval_jaxpr/all_gather | solution.py:129
  93.3 12.8 %fusion.184 = (f32[2,12,256]{2,1,0:T(8,128)S(1)}, f32[2,12,256,1024]{3,2,1,0:T(8,128)}) fusion(pred[2,1024]{1,0:T(4,128)(4,1)S(1)} %iota_compare_fusion.2, bf16[2,1024,12,64]{1,3,2,0:T(8,128)(2,1)} %all-gather.21.cloned.1.call-done, bf16[2,256,12,32]{1,3,2,0:T(8,128)(2,1)S(1)} %get-tuple-element.666, bf16[2,256,12,32]{1,3,2,0:T(8,128)(2,1)S(1)} %get-tuple-element.667), kind=kOutput, calls=%fused_computation.16.clone.1 | convolution fusion | flops 825747456 | bytes 29124608 | tf_op jit(solution)/shard_map/while/body/eval_jaxpr/sqhd,skhd->shqk/dot_general | solution.py:52
  106.2 11.4 %fusion.185 = f32[2,12,256]{2,1,0:T(8,128)S(1)} fusion(f32[2,12,256]{2,1,0:T(8,128)S(1)} %get-tuple-element.668, f32[2,12,256,1024]{3,2,1,0:T(8,128)} %get-tuple-element.669, pred[2,1024]{1,0:T(4,128)(4,1)S(1)} %iota_compare_fusion.2), kind=kLoop, calls=%fused_computation.11.clone.1 | loop fusion | flops 25159680 | bytes 25217024 | tf_op jit(solution)/shard_map/while/body/eval_jaxpr/reduce_sum | solution.py:135
  117.6 6.8 all-gather.23.cloned.1.call-done
  124.4 12.8 %fusion.186 = bf16[2,256,12,64]{1,3,2,0:T(8,128)(2,1)S(1)} fusion(f32[2,12,256]{2,1,0:T(8,128)S(1)} %fusion.185, f32[2,12,256]{2,1,0:T(8,128)S(1)} %get-tuple-element.668, f32[2,12,256,1024]{3,2,1,0:T(8,128)} %get-tuple-element.669, pred[2,1024]{1,0:T(4,128)(4,1)S(1)} %iota_compare_fusion.2, ...), kind=kOutput, calls=%fused_computation.69.clone.1 | convolution fusion | flops 837156864 | bytes 29149184 | tf_op jit(solution)/shard_map/while/body/eval_jaxpr/shqk,skhd->sqhd/dot_general | solution.py:138
  139.1 4.8 all-gather.25.cloned.1.call-done
  148.6 28.0 %all-gather.27.cloned.1.call-done = bf16[768,2304]{1,0:T(8,128)(2,1)} async-done(((bf16[192,2304]{1,0:T(8,128)(2,1)}), bf16[768,2304]{1,0:T(8,128)(2,1)}) %all-gather.27.cloned.1.call-update) | async-done | bytes 3538960 | tf_op jit(solution)/shard_map/while/body/eval_jaxpr/all_gather | solution.py:112
  176.7 6.4 fusion.189
  183.0 16.4 %all-gather.29.cloned.1.call-done = bf16[1152,768]{1,0:T(8,128)(2,1)} async-done(((bf16[288,768]{1,0:T(8,128)(2,1)}), bf16[1152,768]{1,0:T(8,128)(2,1)}) %all-gather.29.cloned.1.call-update) | async-done | bytes 1769488 | tf_op jit(solution)/shard_map/while/body/eval_jaxpr/all_gather | solution.py:158
  199.5 6.4 fusion.192
  218.7 19.6 %multiply_reduce_fusion.9 = (f32[2,12,256]{2,1,0:T(8,128)}, f32[2,12,256,1024]{3,2,1,0:T(8,128)}) fusion(f32[2,12,256]{2,1,0:T(8,128)} %log_add_fusion.2, f32[2,12,256,1024]{3,2,1,0:T(8,128)} %get-tuple-element.669, pred[2,1024]{1,0:T(4,128)(4,1)S(1)} %iota_compare_fusion.2, bf16[2,1024,1,12,64]{1,4,3,2,0:T(8,128)(2,1)} %all-gather.23.cloned.1.call-done, ...), kind=kOutput, calls=%fused_computation.6.clone.1 | convolution fusion | flops 836757504 | bytes 54315008 | tf_op jit(solution)/shard_map/while/body/eval_jaxpr/sqhd,skhd->shqk/dot_general | solution.py:193
  238.2 16.9 %multiply_convert_fusion.13 = bf16[2,12,256,1024]{3,2,1,0:T(8,128)(2,1)S(1)} fusion(f32[2,12,256,1024]{3,2,1,0:T(8,128)} %get-tuple-element.681, f32[2,12,256]{2,1,0:T(8,128)} %get-tuple-element.682, f32[2,12,256]{2,1,0:T(8,128)} %log_add_fusion.2, f32[2,12,256,1024]{3,2,1,0:T(8,128)} %get-tuple-element.669, pred[2,1024]{1,0:T(4,128)(4,1)S(1)} %iota_compare_fusion.2), kind=kLoop, calls=%fused_computation.5.clone.1 | loop fusion | flops 37748736 | bytes 62965760 | tf_op jit(solution)/shard_map/while/body/eval_jaxpr/convert_element_type | solution.py:197
  264.4 14.4 %convert_bitcast_fusion.2 = bf16[2,1024,12,64]{1,3,2,0:T(8,128)(2,1)} fusion(f32[2,12,256]{2,1,0:T(8,128)S(1)} %copy-done.37, f32[2,12,256,1024]{3,2,1,0:T(8,128)} %get-tuple-element.669, pred[2,1024]{1,0:T(4,128)(4,1)S(1)} %iota_compare_fusion.2, bf16[2,256,12,64]{1,0,3,2:T(2,128)(2,1)} %reshape.379), kind=kOutput, calls=%fused_computation.27.clone.1 | convolution fusion | flops 832045056 | bytes 29124608 | tf_op jit(solution)/shard_map/while/body/eval_jaxpr/shqk,sqhd->skhd/dot_general | solution.py:206
  293.4 5.2 select_add_fusion.8
  298.7 8.6 multiply_bitcast_fusion.2
  309.2 33.2 %reduce-scatter.20.cloned.1.call-done = bf16[2,256,12,64]{1,3,2,0:T(8,128)(2,1)} async-done(((bf16[2,1024,12,64]{1,3,2,0:T(8,128)(2,1)}), bf16[2,256,12,64]{1,3,2,0:T(8,128)(2,1)}) %reduce-scatter.20.cloned.1.call-update) | async-done | bytes 786448 | tf_op jit(solution)/shard_map/while/body/eval_jaxpr/reduce_scatter | solution.py:213
  363.1 5.1 all-gather.10
  370.6 25.4 %all-gather.19.cloned.1.call-done = bf16[768,2304]{1,0:T(8,128)(2,1)} async-done(((bf16[192,2304]{1,0:T(8,128)(2,1)}), bf16[768,2304]{1,0:T(8,128)(2,1)}) %all-gather.19.cloned.1.call-update) | async-done | bytes 3538960 | tf_op jit(solution)/shard_map/while/body/eval_jaxpr/all_gather | solution.py:110
  396.0 5.8 copy.94
  419.1 19.6 %all-gather.21.cloned.1.call-done = bf16[2,1024,12,64]{1,3,2,0:T(8,128)(2,1)} async-done(((bf16[2,256,12,64]{1,3,2,0:T(8,128)(2,1)}), bf16[2,1024,12,64]{1,3,2,0:T(8,128)(2,1)}) %all-gather.21.cloned.1.call-update) | async-done | bytes 3145744 | tf_op jit(solution)/shard_map/while/body/eval_jaxpr/all_gather | solution.py:129
  438.8 12.8 %fusion.184 = (f32[2,12,256]{2,1,0:T(8,128)S(1)}, f32[2,12,256,1024]{3,2,1,0:T(8,128)}) fusion(pred[2,1024]{1,0:T(4,128)(4,1)S(1)} %iota_compare_fusion.2, bf16[2,1024,12,64]{1,3,2,0:T(8,128)(2,1)} %all-gather.21.cloned.1.call-done, bf16[2,256,12,32]{1,3,2,0:T(8,128)(2,1)S(1)} %get-tuple-element.666, bf16[2,256,12,32]{1,3,2,0:T(8,128)(2,1)S(1)} %get-tuple-element.667), kind=kOutput, calls=%fused_computation.16.clone.1 | convolution fusion | flops 825747456 | bytes 29124608 | tf_op jit(solution)/shard_map/while/body/eval_jaxpr/sqhd,skhd->shqk/dot_general | solution.py:52
  451.6 11.4 %fusion.185 = f32[2,12,256]{2,1,0:T(8,128)S(1)} fusion(f32[2,12,256]{2,1,0:T(8,128)S(1)} %get-tuple-element.668, f32[2,12,256,1024]{3,2,1,0:T(8,128)} %get-tuple-element.669, pred[2,1024]{1,0:T(4,128)(4,1)S(1)} %iota_compare_fusion.2), kind=kLoop, calls=%fused_computation.11.clone.1 | loop fusion | flops 25159680 | bytes 25217024 | tf_op jit(solution)/shard_map/while/body/eval_jaxpr/reduce_sum | solution.py:135
  463.0 6.9 all-gather.23.cloned.1.call-done
  469.9 12.6 %fusion.186 = bf16[2,256,12,64]{1,3,2,0:T(8,128)(2,1)S(1)} fusion(f32[2,12,256]{2,1,0:T(8,128)S(1)} %fusion.185, f32[2,12,256]{2,1,0:T(8,128)S(1)} %get-tuple-element.668, f32[2,12,256,1024]{3,2,1,0:T(8,128)} %get-tuple-element.669, pred[2,1024]{1,0:T(4,128)(4,1)S(1)} %iota_compare_fusion.2, ...), kind=kOutput, calls=%fused_computation.69.clone.1 | convolution fusion | flops 837156864 | bytes 29149184 | tf_op jit(solution)/shard_map/while/body/eval_jaxpr/shqk,skhd->sqhd/dot_general | solution.py:138
  484.4 5.0 all-gather.25.cloned.1.call-done
  494.1 28.2 %all-gather.27.cloned.1.call-done = bf16[768,2304]{1,0:T(8,128)(2,1)} async-done(((bf16[192,2304]{1,0:T(8,128)(2,1)}), bf16[768,2304]{1,0:T(8,128)(2,1)}) %all-gather.27.cloned.1.call-update) | async-done | bytes 3538960 | tf_op jit(solution)/shard_map/while/body/eval_jaxpr/all_gather | solution.py:112
  522.3 6.4 fusion.189
  528.7 16.4 %all-gather.29.cloned.1.call-done = bf16[1152,768]{1,0:T(8,128)(2,1)} async-done(((bf16[288,768]{1,0:T(8,128)(2,1)}), bf16[1152,768]{1,0:T(8,128)(2,1)}) %all-gather.29.cloned.1.call-update) | async-done | bytes 1769488 | tf_op jit(solution)/shard_map/while/body/eval_jaxpr/all_gather | solution.py:158
  545.1 6.4 fusion.192
  564.3 19.8 %multiply_reduce_fusion.9 = (f32[2,12,256]{2,1,0:T(8,128)}, f32[2,12,256,1024]{3,2,1,0:T(8,128)}) fusion(f32[2,12,256]{2,1,0:T(8,128)} %log_add_fusion.2, f32[2,12,256,1024]{3,2,1,0:T(8,128)} %get-tuple-element.669, pred[2,1024]{1,0:T(4,128)(4,1)S(1)} %iota_compare_fusion.2, bf16[2,1024,1,12,64]{1,4,3,2,0:T(8,128)(2,1)} %all-gather.23.cloned.1.call-done, ...), kind=kOutput, calls=%fused_computation.6.clone.1 | convolution fusion | flops 836757504 | bytes 54315008 | tf_op jit(solution)/shard_map/while/body/eval_jaxpr/sqhd,skhd->shqk/dot_general | solution.py:193
  584.1 16.9 %multiply_convert_fusion.13 = bf16[2,12,256,1024]{3,2,1,0:T(8,128)(2,1)S(1)} fusion(f32[2,12,256,1024]{3,2,1,0:T(8,128)} %get-tuple-element.681, f32[2,12,256]{2,1,0:T(8,128)} %get-tuple-element.682, f32[2,12,256]{2,1,0:T(8,128)} %log_add_fusion.2, f32[2,12,256,1024]{3,2,1,0:T(8,128)} %get-tuple-element.669, pred[2,1024]{1,0:T(4,128)(4,1)S(1)} %iota_compare_fusion.2), kind=kLoop, calls=%fused_computation.5.clone.1 | loop fusion | flops 37748736 | bytes 62965760 | tf_op jit(solution)/shard_map/while/body/eval_jaxpr/convert_element_type | solution.py:197
  610.3 14.3 %convert_bitcast_fusion.2 = bf16[2,1024,12,64]{1,3,2,0:T(8,128)(2,1)} fusion(f32[2,12,256]{2,1,0:T(8,128)S(1)} %copy-done.37, f32[2,12,256,1024]{3,2,1,0:T(8,128)} %get-tuple-element.669, pred[2,1024]{1,0:T(4,128)(4,1)S(1)} %iota_compare_fusion.2, bf16[2,256,12,64]{1,0,3,2:T(2,128)(2,1)} %reshape.379), kind=kOutput, calls=%fused_computation.27.clone.1 | convolution fusion | flops 832045056 | bytes 29124608 | tf_op jit(solution)/shard_map/while/body/eval_jaxpr/shqk,sqhd->skhd/dot_general | solution.py:206
  639.2 8.4 select_add_fusion.8
  647.6 8.5 multiply_bitcast_fusion.2
  658.1 30.1 %reduce-scatter.20.cloned.1.call-done = bf16[2,256,12,64]{1,3,2,0:T(8,128)(2,1)} async-done(((bf16[2,1024,12,64]{1,3,2,0:T(8,128)(2,1)}), bf16[2,256,12,64]{1,3,2,0:T(8,128)(2,1)}) %reduce-scatter.20.cloned.1.call-update) | async-done | bytes 786448 | tf_op jit(solution)/shard_map/while/body/eval_jaxpr/reduce_scatter | solution.py:213
  718.7 5.1 convert_element_type.212
  723.9 5.1 convert_element_type.216
  729.1 6.6 reduce-scatter.18.cloned.1.call-done
  736.6 27.8 %reduce-scatter.12.cloned.1.call-done = bf16[192,768]{1,0:T(8,128)(2,1)} async-done(((bf16[768,768]{1,0:T(8,128)(2,1)}), bf16[192,768]{1,0:T(8,128)(2,1)}) %reduce-scatter.12.cloned.1.call-update) | async-done | bytes 294928 | tf_op jit(solution)/shard_map/reduce_scatter | solution.py:247
  764.4 32.5 %reduce-scatter.16.cloned.1.call-done = bf16[288,768]{1,0:T(8,128)(2,1)} async-done(((bf16[1152,768]{1,0:T(8,128)(2,1)}), bf16[288,768]{1,0:T(8,128)(2,1)}) %reduce-scatter.16.cloned.1.call-update) | async-done | bytes 442384 | tf_op jit(solution)/shard_map/reduce_scatter | solution.py:253
  797.0 42.9 %reduce-scatter.10.cloned.1.call-done = bf16[192,2304]{1,0:T(8,128)(2,1)} async-done(((bf16[768,2304]{1,0:T(8,128)(2,1)}), bf16[192,2304]{1,0:T(8,128)(2,1)}) %reduce-scatter.10.cloned.1.call-update) | async-done | bytes 884752 | tf_op jit(solution)/shard_map/reduce_scatter | solution.py:244
  839.9 43.1 %reduce-scatter.14.cloned.1.call-done = bf16[192,2304]{1,0:T(8,128)(2,1)} async-done(((bf16[768,2304]{1,0:T(8,128)(2,1)}), bf16[192,2304]{1,0:T(8,128)(2,1)}) %reduce-scatter.14.cloned.1.call-update) | async-done | bytes 884752 | tf_op jit(solution)/shard_map/reduce_scatter | solution.py:250
  882.9 199.7 %all-reduce.4 = (f32[192,2304]{1,0:T(8,128)}, f32[192,768]{1,0:T(8,128)}, f32[192,2304]{1,0:T(8,128)}, f32[288,768]{1,0:T(8,128)}, f32[2,192]{1,0:T(2,128)S(1)}) all-reduce(bf16[192,2304]{1,0:T(8,128)(2,1)} %reduce-scatter.10.cloned.1.call-done, ...), channel_id=1, replica_groups=mesh['dp'=8,'fsdp'=4] {'dp'}, use_global_device_ids=true, to_apply=%region_18.19 | all-reduce | flops 1253760 | bytes 7522560 | tf_op jit(solution)/shard_map/psum | solution.py:260
  1089.9 6.5 multiply_subtract_fusion.2
  (482 shorter events, 189.4 us)
Async XLA Ops:
  14.0 9.4 copy-start.31
  14.0 9.4 copy-start.63
  14.0 9.4 copy-start.66
  14.0 9.4 copy-start.68
  14.0 36.5 %all-gather.19.cloned.1.call-start = ((), (), s32[]{:S(2)}) async-start(), calls=%async_computation.12 | async-start | bytes 4423680 | tf_op jit(solution)/shard_map/while/body/eval_jaxpr/all_gather | solution.py:110
  14.9 78.4 %all-gather.21.cloned.1.call-start = ((), (), s32[]{:S(2)}) async-start(), calls=%async_computation.13 | async-start | bytes 3932160 | tf_op jit(solution)/shard_map/while/body/eval_jaxpr/all_gather | solution.py:129
  21.3 35.0 %copy-start.50 = (f32[768]{0:T(1024)}, f32[768]{0:T(1024)S(1)}, u32[]{:S(2)}) copy-start(f32[768]{0:T(1024)S(1)} %get-tuple-element.657) | copy-start | bytes 9220 | tf_op jit(solution)/shard_map/while
  23.0 39.5 %copy-start.33 = (f32[256,32]{0,1:T(8,128)}, f32[256,32]{0,1:T(8,128)S(1)}, u32[]{:S(2)}) copy-start(f32[256,32]{0,1:T(8,128)S(1)} %get-tuple-element.662) | copy-start | bytes 98308 | tf_op jit(solution)/shard_map/while
  23.4 32.9 %copy-start.9 = (bf16[1,2,256,768]{3,2,1,0:T(8,128)(2,1)}, bf16[1,2,256,768]{3,2,1,0:T(8,128)(2,1)S(1)}, u32[]{:S(2)}) copy-start(bf16[1,2,256,768]{3,2,1,0:T(8,128)(2,1)S(1)} %fusion.181) | copy-start | bytes 2359300 | tf_op jit(solution)/shard_map/while
  63.1 30.2 %copy-start.14 = (bf16[2,256,12,32]{1,3,2,0:T(8,128)(2,1)}, bf16[2,256,12,32]{1,3,2,0:T(8,128)(2,1)S(1)}, u32[]{:S(2)}) copy-start(bf16[2,256,12,32]{1,3,2,0:T(8,128)(2,1)S(1)} %get-tuple-element.666) | copy-start | bytes 1179652 | tf_op jit(solution)/shard_map/while
  64.2 60.2 %all-gather.23.cloned.1.call-start = ((), (), s32[]{:S(2)}) async-start(), calls=%async_computation.14 | async-start | bytes 3932160 | tf_op jit(solution)/shard_map/while/body/eval_jaxpr/all_gather | solution.py:130
  66.6 77.3 %all-gather.25.cloned.1.call-start = ((), (), s32[]{:S(2)}) async-start(), calls=%async_computation.15 | async-start | bytes 1474560 | tf_op jit(solution)/shard_map/while/body/eval_jaxpr/all_gather | solution.py:111
  67.2 109.5 %all-gather.27.cloned.1.call-start = ((), (), s32[]{:S(2)}) async-start(), calls=%async_computation.16 | async-start | bytes 4423680 | tf_op jit(solution)/shard_map/while/body/eval_jaxpr/all_gather | solution.py:112
  67.8 131.7 %all-gather.29.cloned.1.call-start = ((), (), s32[]{:S(2)}) async-start(), calls=%async_computation.17 | async-start | bytes 2211840 | tf_op jit(solution)/shard_map/while/body/eval_jaxpr/all_gather | solution.py:158
  68.4 238.9 %reduce-scatter.22.cloned.1.call-start = ((), (), s32[]{:S(2)}) async-start(), calls=%async_computation.19 | async-start | bytes 3932160 | tf_op jit(solution)/shard_map/while/body/eval_jaxpr/reduce_scatter | solution.py:210
  106.2 18.3 %copy-start.35 = (f32[2,12,256]{2,1,0:T(8,128)}, f32[2,12,256]{2,1,0:T(8,128)S(1)}, u32[]{:S(2)}) copy-start(f32[2,12,256]{2,1,0:T(8,128)S(1)} %get-tuple-element.668) | copy-start | bytes 73732 | tf_op jit(solution)/shard_map/while
  117.6 19.7 %copy-start.43 = (f32[2,12,256]{2,1,0:T(8,128)}, f32[2,12,256]{2,1,0:T(8,128)S(1)}, u32[]{:S(2)}) copy-start(f32[2,12,256]{2,1,0:T(8,128)S(1)} %fusion.185) | copy-start | bytes 73732 | tf_op jit(solution)/shard_map/while
  238.2 21.5 %copy-start.15 = (bf16[2,256,12,32]{1,3,2,0:T(8,128)(2,1)S(1)}, bf16[2,256,12,32]{1,3,2,0:T(8,128)(2,1)}, u32[]{:S(2)}) copy-start(bf16[2,256,12,32]{1,3,2,0:T(8,128)(2,1)} %copy-done.14) | copy-start | bytes 1179652 | tf_op jit(solution)/shard_map/while
  263.7 78.8 %reduce-scatter.20.cloned.1.call-start = ((), (), s32[]{:S(2)}) async-start(), calls=%async_computation.18 | async-start | bytes 3932160 | tf_op jit(solution)/shard_map/while/body/eval_jaxpr/reduce_scatter | solution.py:213
  343.9 10.8 slice-start
  362.2 8.4 copy-start.31
  362.2 33.8 %all-gather.19.cloned.1.call-start = ((), (), s32[]{:S(2)}) async-start(), calls=%async_computation.12 | async-start | bytes 4423680 | tf_op jit(solution)/shard_map/while/body/eval_jaxpr/all_gather | solution.py:110
  363.1 75.7 %all-gather.21.cloned.1.call-start = ((), (), s32[]{:S(2)}) async-start(), calls=%async_computation.13 | async-start | bytes 3932160 | tf_op jit(solution)/shard_map/while/body/eval_jaxpr/all_gather | solution.py:129
  368.5 33.2 %copy-start.50 = (f32[768]{0:T(1024)}, f32[768]{0:T(1024)S(1)}, u32[]{:S(2)}) copy-start(f32[768]{0:T(1024)S(1)} %get-tuple-element.657) | copy-start | bytes 9220 | tf_op jit(solution)/shard_map/while
  370.3 37.8 %copy-start.33 = (f32[256,32]{0,1:T(8,128)}, f32[256,32]{0,1:T(8,128)S(1)}, u32[]{:S(2)}) copy-start(f32[256,32]{0,1:T(8,128)S(1)} %get-tuple-element.662) | copy-start | bytes 98308 | tf_op jit(solution)/shard_map/while
  370.6 31.1 %copy-start.9 = (bf16[1,2,256,768]{3,2,1,0:T(8,128)(2,1)}, bf16[1,2,256,768]{3,2,1,0:T(8,128)(2,1)S(1)}, u32[]{:S(2)}) copy-start(bf16[1,2,256,768]{3,2,1,0:T(8,128)(2,1)S(1)} %fusion.181) | copy-start | bytes 2359300 | tf_op jit(solution)/shard_map/while
  408.6 30.1 %copy-start.14 = (bf16[2,256,12,32]{1,3,2,0:T(8,128)(2,1)}, bf16[2,256,12,32]{1,3,2,0:T(8,128)(2,1)S(1)}, u32[]{:S(2)}) copy-start(bf16[2,256,12,32]{1,3,2,0:T(8,128)(2,1)S(1)} %get-tuple-element.666) | copy-start | bytes 1179652 | tf_op jit(solution)/shard_map/while
  409.7 60.2 %all-gather.23.cloned.1.call-start = ((), (), s32[]{:S(2)}) async-start(), calls=%async_computation.14 | async-start | bytes 3932160 | tf_op jit(solution)/shard_map/while/body/eval_jaxpr/all_gather | solution.py:130
  412.2 77.2 %all-gather.25.cloned.1.call-start = ((), (), s32[]{:S(2)}) async-start(), calls=%async_computation.15 | async-start | bytes 1474560 | tf_op jit(solution)/shard_map/while/body/eval_jaxpr/all_gather | solution.py:111
  412.7 109.6 %all-gather.27.cloned.1.call-start = ((), (), s32[]{:S(2)}) async-start(), calls=%async_computation.16 | async-start | bytes 4423680 | tf_op jit(solution)/shard_map/while/body/eval_jaxpr/all_gather | solution.py:112
  413.5 131.6 %all-gather.29.cloned.1.call-start = ((), (), s32[]{:S(2)}) async-start(), calls=%async_computation.17 | async-start | bytes 2211840 | tf_op jit(solution)/shard_map/while/body/eval_jaxpr/all_gather | solution.py:158
  414.1 242.1 %reduce-scatter.22.cloned.1.call-start = ((), (), s32[]{:S(2)}) async-start(), calls=%async_computation.19 | async-start | bytes 3932160 | tf_op jit(solution)/shard_map/while/body/eval_jaxpr/reduce_scatter | solution.py:210
  451.6 18.3 %copy-start.35 = (f32[2,12,256]{2,1,0:T(8,128)}, f32[2,12,256]{2,1,0:T(8,128)S(1)}, u32[]{:S(2)}) copy-start(f32[2,12,256]{2,1,0:T(8,128)S(1)} %get-tuple-element.668) | copy-start | bytes 73732 | tf_op jit(solution)/shard_map/while
  463.0 19.5 %copy-start.43 = (f32[2,12,256]{2,1,0:T(8,128)}, f32[2,12,256]{2,1,0:T(8,128)S(1)}, u32[]{:S(2)}) copy-start(f32[2,12,256]{2,1,0:T(8,128)S(1)} %fusion.185) | copy-start | bytes 73732 | tf_op jit(solution)/shard_map/while
  584.1 21.5 %copy-start.15 = (bf16[2,256,12,32]{1,3,2,0:T(8,128)(2,1)S(1)}, bf16[2,256,12,32]{1,3,2,0:T(8,128)(2,1)}, u32[]{:S(2)}) copy-start(bf16[2,256,12,32]{1,3,2,0:T(8,128)(2,1)} %copy-done.14) | copy-start | bytes 1179652 | tf_op jit(solution)/shard_map/while
  609.6 78.6 %reduce-scatter.20.cloned.1.call-start = ((), (), s32[]{:S(2)}) async-start(), calls=%async_computation.18 | async-start | bytes 3932160 | tf_op jit(solution)/shard_map/while/body/eval_jaxpr/reduce_scatter | solution.py:213
  689.6 10.6 slice-start
  712.5 23.2 %reduce-scatter.18.cloned.1.call-start = ((), (), s32[]{:S(2)}) async-start(), calls=%async_computation.11 | async-start | bytes 245760
  714.2 50.3 %reduce-scatter.12.cloned.1.call-start = ((), (), s32[]{:S(2)}) async-start(), calls=%async_computation.8 | async-start | bytes 1474560 | tf_op jit(solution)/shard_map/reduce_scatter | solution.py:247
  717.2 79.8 %reduce-scatter.16.cloned.1.call-start = ((), (), s32[]{:S(2)}) async-start(), calls=%async_computation.10 | async-start | bytes 2211840 | tf_op jit(solution)/shard_map/reduce_scatter | solution.py:253
  718.7 121.2 %reduce-scatter.10.cloned.1.call-start = ((), (), s32[]{:S(2)}) async-start(), calls=%async_computation.7 | async-start | bytes 4423680 | tf_op jit(solution)/shard_map/reduce_scatter | solution.py:244
  723.9 159.0 %reduce-scatter.14.cloned.1.call-start = ((), (), s32[]{:S(2)}) async-start(), calls=%async_computation.9 | async-start | bytes 4423680 | tf_op jit(solution)/shard_map/reduce_scatter | solution.py:250
  729.1 357.2 %copy-start.52 = (f32[288,768]{1,0:T(8,128)S(1)}, f32[288,768]{1,0:T(8,128)}, u32[]{:S(2)}) copy-start(f32[288,768]{1,0:T(8,128)} %param.31) | copy-start | bytes 2654212
  729.1 353.5 %copy-start.70 = (f32[2,192]{1,0:T(2,128)S(1)}, f32[2,192]{1,0:T(2,128)}, u32[]{:S(2)}) copy-start(f32[2,192]{1,0:T(2,128)} %param.27) | copy-start | bytes 4612
  729.1 353.5 %copy-start.71 = (f32[2,192]{1,0:T(2,128)S(1)}, f32[2,192]{1,0:T(2,128)}, u32[]{:S(2)}) copy-start(f32[2,192]{1,0:T(2,128)} %param.32) | copy-start | bytes 4612
  729.1 353.5 %copy-start.72 = (f32[2,192]{1,0:T(2,128)S(1)}, f32[2,192]{1,0:T(2,128)}, u32[]{:S(2)}) copy-start(f32[2,192]{1,0:T(2,128)} %param.37) | copy-start | bytes 4612
  729.1 354.1 %copy-start.45 = (f32[192,768]{1,0:T(8,128)S(1)}, f32[192,768]{1,0:T(8,128)}, u32[]{:S(2)}) copy-start(f32[192,768]{1,0:T(8,128)} %param.24) | copy-start | bytes 1769476
  882.9 207.0 %copy-start.49 = (f32[192,2304]{1,0:T(8,128)S(1)}, f32[192,2304]{1,0:T(8,128)}, u32[]{:S(2)}) copy-start(f32[192,2304]{1,0:T(8,128)} %param.28) | copy-start | bytes 5308420
  (119 other events, 389.5 us)
Sparse Core Ops, SparseCore 0:
  17.0 33.4 all-gather.18
  64.3 28.9 all-gather.20
  95.4 28.9 all-gather.22
  126.4 17.4 all-gather.24
  145.9 30.7 all-gather.26
  178.7 20.7 all-gather.28
  263.8 37.9 reduce-scatter.21
  304.5 37.9 reduce-scatter.19
  365.2 30.7 all-gather.18
  409.8 28.9 all-gather.20
  440.9 28.9 all-gather.22
  471.9 17.4 all-gather.24
  491.5 30.7 all-gather.26
  524.3 20.7 all-gather.28
  609.7 37.9 reduce-scatter.21
  650.3 37.9 reduce-scatter.19
Sparse Core Ops, SparseCore 1:
  716.0 19.7 reduce-scatter.17
  738.8 25.6 reduce-scatter.11
  767.7 29.3 reduce-scatter.15
  799.6 40.2 reduce-scatter.9
  842.6 40.2 reduce-scatter.13
where the time goes:
time: 1110 us; the launch traced here: 1100 us
  waiting for transfers between devices  424 us (38%)
  matrix products  233 us (21%)
  blocking collectives  211 us (19%)
  other arithmetic  118 us (11%)
  local copies, waits for them, and re-layouts  94.6 us (9%)
  between operations  15.9 us (1%)
    psum x1, blocking collectives, local(): lax.psum((shards[0], shards[1], shards[2], shards[3], shards[4]), 'dp')  200 us
    reduce_scatter x2, waiting for transfers between devices, micro_step(): lax.psum_scatter(value_part.astype(jnp.bfloat16), 'fsdp', scatter_dimensi...  63.3 us
    all_gather x2, waiting for transfers between devices, micro_step(): lax.all_gather(expand_copy, 'fsdp', axis=0, tiled=True)  56.2 us
    all_gather x2, waiting for transfers between devices, micro_step(): lax.all_gather(inward_copy, 'fsdp', axis=0, tiled=True)  52.4 us
    while x270, local copies, waits for them, and re-layouts  51.2 us
    reduce_scatter x1, waiting for transfers between devices, local(): lax.psum_scatter(accum[2].astype(jnp.bfloat16), 'fsdp', scatter_dimension...  43.1 us
    reduce_scatter x1, waiting for transfers between devices, local(): lax.psum_scatter(accum[0].astype(jnp.bfloat16), 'fsdp', scatter_dimension...  42.9 us
    all_gather x2, waiting for transfers between devices, micro_step(): lax.all_gather(keys_local, 'fsdp', axis=1, tiled=True)  39.5 us
  transfers between devices with their start and end apart: 21, of which 19 were waited for; matrix products, arithmetic and copies ran while one was open for 19% of the time, Pallas kernels for 0%

commit v1 on v0

--- a/solution.py
+++ b/solution.py
@@ -14,6 +14,40 @@
 weight_decay = 0.01
 rates = (0.07, 2.0, 0.07, 0.06, 0.2)
 masked_score = -1e30
+
+
+def expand_columns(row_data, axis_no):
+    row_data = jnp.moveaxis(row_data, 0, axis_no)
+    lower = row_data.shape
+    t_next = row_data.reshape(
+        *lower[:axis_no], lower[axis_no] * lower[axis_no + 1], *lower[axis_no + 2 :]
+    )
+    return t_next
+
+
+def rest_results(join_dim, shard_axis, mine_x):
+    n_axis = lax.psum(1, shard_axis)
+    xs_all = []
+    for p in range(n_axis):
+        xs_all.append((p, (p + 1) % n_axis))
+    lanes = []
+    for dev_j, u in xs_all:
+        lanes.append((u, dev_j))
+    parts_out, placed = ([], [])
+    for s in range(n_axis - 1):
+        if s % 2 == 0:
+            upper = lax.ppermute(parts_out[-1] if parts_out else mine_x, shard_axis, xs_all)
+            parts_out.append(upper)
+        else:
+            met_up = lax.ppermute(placed[-1] if placed else mine_x, shard_axis, lanes)
+            placed.append(met_up)
+    response = jnp.stack([*parts_out[::-1], mine_x, *placed])
+    reached = lax.axis_index(shard_axis)
+    plain = len(parts_out)
+    big = reached - plain
+    response = response[(jnp.arange(n_axis) - big) % n_axis]
+    back = expand_columns(response, join_dim)
+    return back
 
 
 def tables(positions):
@@ -126,7 +160,7 @@
         keys_local = rotate(joined_heads[:, :, 1], cosine, sine_table).astype(jnp.bfloat16)
         values_local = joined_heads[:, :, 2].astype(jnp.bfloat16)
         keys_all, values_all = (
-            lax.all_gather(keys_local, "fsdp", axis=1, tiled=True),
+            rest_results(1, "fsdp", keys_local),
             lax.all_gather(values_local, "fsdp", axis=1, tiled=True),
         )
         scores = attention_scores(queries, keys_all, live_keys, score_scale)

time: 1110 us -> 1070 us (0.964)
  waiting for transfers between devices: 424 us -> 369 us
    ppermute x0 -> x6, waiting for transfers between devices: none -> 80.9 us  [the longest x4 80.9 us: rest_results(): lax.ppermute(parts_out[-1] if parts_out else mine_x, shard_axis, xs_all)]
    all_gather x2, waiting for transfers between devices: 56.2 us -> 0.01 us  [micro_step(): lax.all_gather(expand_copy, 'fsdp', axis=0, tiled=True)]
    all_gather x2 -> x0, waiting for transfers between devices: 39.5 us -> none  [micro_step(): lax.all_gather(keys_local, 'fsdp', axis=1, tiled=True)]
    all_gather x2, waiting for transfers between devices: 13.7 us -> 0.01 us  [micro_step(): lax.all_gather(values_local, 'fsdp', axis=1, tiled=True)]
    while x270 -> x286, local copies, waits for them, and re-layouts: 51.2 us -> 49 us
  transfers between devices with their start and end apart: 21 -> 25, of which waited for: 19 -> 15; matrix products, arithmetic and copies ran while one was open for 19% -> 22% of each run, Pallas kernels for 0% -> 0%
where the time goes in v1:
time: 1070 us
  waiting for transfers between devices  369 us (34%)
  matrix products  236 us (22%)
  blocking collectives  211 us (20%)
  other arithmetic  126 us (12%)
  local copies, waits for them, and re-layouts  101 us (9%)
  between operations  15.8 us (1%)
    psum x1, blocking collectives, local(): lax.psum((shards[0], shards[1], shards[2], shards[3], shards[4]), 'dp')  200 us
    ppermute x4, waiting for transfers between devices, rest_results(): lax.ppermute(parts_out[-1] if parts_out else mine_x, shard_axis, xs_all)  80.9 us
    reduce_scatter x2, waiting for transfers between devices, micro_step(): lax.psum_scatter(value_part.astype(jnp.bfloat16), 'fsdp', scatter_dimensi...  59.4 us
    all_gather x2, waiting for transfers between devices, micro_step(): lax.all_gather(inward_copy, 'fsdp', axis=0, tiled=True)  52.4 us
    while x286, local copies, waits for them, and re-layouts  49 us
    reduce_scatter x1, waiting for transfers between devices, local(): lax.psum_scatter(accum[2].astype(jnp.bfloat16), 'fsdp', scatter_dimension...  43.1 us
    reduce_scatter x1, waiting for transfers between devices, local(): lax.psum_scatter(accum[0].astype(jnp.bfloat16), 'fsdp', scatter_dimension...  42.9 us
    dot_general x2, matrix products, micro_step(): jnp.einsum('sqhd,skhd->shqk', mixed_grad, values_all, preferred_element_t...  39.3 us
  transfers between devices with their start and end apart: 25, of which 15 were waited for; matrix products, arithmetic and copies ran while one was open for 22% of the time, Pallas kernels for 0%

profile of v1, /device:TPU:0, one launch (start us, length us, event | category | flops | bytes accessed | tf_op | source)
XLA Modules:
  0.0 1070.3 jit_solution(12357917258198014570)
XLA Ops:
  14.6 664.4 %while.27 = (s32[]{:T(128)}, f32[768,2304]{1,0:T(8,128)}, f32[768,768]{1,0:T(8,128)}, f32[768,2304]{1,0:T(8,128)}, f32[1152,768]{1,0:T(8,128)}, /*index=5*/f32[2...) while((s32[]{:T(128)}, f32[768,2304]{1,0:T(8,128)}, ...), condition=%wide.region_16.17_spmd.clone.clone.clone, body=%wide.region_0.16_spmd.clone.clone.clone.sunk | while | flops 20497588224 | bytes 911273408 | solution.py:275
  15.6 6.3 all-gather.10
  24.0 27.0 %all-gather.18.cloned.1.call-done = bf16[768,2304]{1,0:T(8,128)(2,1)} async-done(((bf16[192,2304]{1,0:T(8,128)(2,1)}), bf16[768,2304]{1,0:T(8,128)(2,1)}) %all-gather.18.cloned.1.call-update) | async-done | bytes 3538960 | tf_op jit(solution)/shard_map/while/body/eval_jaxpr/all_gather | solution.py:144
  51.1 5.7 copy.99
  72.3 32.6 %collective-permute-done.1 = bf16[2,256,12,64]{1,3,2,0:T(8,128)(2,1)S(1)} collective-permute-done((bf16[2,256,12,64]{1,3,2,0:T(8,128)(2,1)}, bf16[2,256,12,64]{1,3,2,0:T(8,128)(2,1)S(1)}, u32[]{:S(2)}, u32[]{:S(2)}) %collective-permute-start.1) | collective-permute-done | bytes 786464 | tf_op jit(solution)/shard_map/while/body/eval_jaxpr/ppermute | solution.py:39
  108.6 7.8 collective-permute-done.2
  122.5 10.3 fusion.188
  132.8 12.0 %fusion.189 = f32[2,12,256]{2,1,0:T(8,128)S(1)} fusion(f32[2,12,256]{2,1,0:T(8,128)S(1)} %get-tuple-element.734, f32[2,12,256,1024]{3,2,1,0:T(8,128)} %get-tuple-element.735, pred[2,1024]{1,0:T(4,128)(4,1)S(1)} %iota_compare_fusion.2), kind=kLoop, calls=%fused_computation.12.clone.1 | loop fusion | flops 25159680 | bytes 25217024 | tf_op jit(solution)/shard_map/while/body/eval_jaxpr/reduce_sum | solution.py:169
  146.1 12.8 %fusion.190 = bf16[2,256,12,64]{1,3,2,0:T(8,128)(2,1)S(1)} fusion(f32[2,12,256]{2,1,0:T(8,128)} %copy-done.48, f32[2,12,256]{2,1,0:T(8,128)} %copy-done.41, f32[2,12,256,1024]{3,2,1,0:T(8,128)} %get-tuple-element.735, pred[2,1024]{1,0:T(4,128)(4,1)S(1)} %iota_compare_fusion.2, bf16[2,1024,1,12,64]{1,4,3,2,0:T(8,128)(2,1)} %all-gather.20.cloned.1.call-done), kind=kOutput, calls=%fused_computation.71.clone.1 | convolution fusion | flops 837156864 | bytes 29149184 | tf_op jit(solution)/shard_map/while/body/eval_jaxpr/shqk,skhd->sqhd/dot_general | solution.py:172
  166.0 6.8 fusion.193
  172.8 11.1 %all-gather.26.cloned.1.call-done = bf16[1152,768]{1,0:T(8,128)(2,1)} async-done(((bf16[288,768]{1,0:T(8,128)(2,1)}), bf16[1152,768]{1,0:T(8,128)(2,1)}) %all-gather.26.cloned.1.call-update) | async-done | bytes 1769488 | tf_op jit(solution)/shard_map/while/body/eval_jaxpr/all_gather | solution.py:192
  183.9 6.4 fusion.196
  203.1 19.5 %multiply_reduce_fusion.9 = (f32[2,12,256]{2,1,0:T(8,128)}, f32[2,12,256,1024]{3,2,1,0:T(8,128)}) fusion(f32[2,12,256]{2,1,0:T(8,128)} %log_add_fusion.2, f32[2,12,256,1024]{3,2,1,0:T(8,128)} %get-tuple-element.735, pred[2,1024]{1,0:T(4,128)(4,1)S(1)} %iota_compare_fusion.2, bf16[2,1024,1,12,64]{1,4,3,2,0:T(8,128)(2,1)} %all-gather.20.cloned.1.call-done, ...), kind=kOutput, calls=%fused_computation.7.clone.1 | convolution fusion | flops 836757504 | bytes 54315008 | tf_op jit(solution)/shard_map/while/body/eval_jaxpr/sqhd,skhd->shqk/dot_general | solution.py:227
  222.6 16.9 %multiply_convert_fusion.13 = bf16[2,12,256,1024]{3,2,1,0:T(8,128)(2,1)S(1)} fusion(f32[2,12,256,1024]{3,2,1,0:T(8,128)} %get-tuple-element.747, f32[2,12,256]{2,1,0:T(8,128)} %get-tuple-element.748, f32[2,12,256]{2,1,0:T(8,128)} %log_add_fusion.2, f32[2,12,256,1024]{3,2,1,0:T(8,128)} %get-tuple-element.735, pred[2,1024]{1,0:T(4,128)(4,1)S(1)} %iota_compare_fusion.2), kind=kLoop, calls=%fused_computation.6.clone.1 | loop fusion | flops 37748736 | bytes 62965760 | tf_op jit(solution)/shard_map/while/body/eval_jaxpr/convert_element_type | solution.py:231
  239.5 4.6 copy-done
  248.8 14.4 %convert_bitcast_fusion.2 = bf16[2,1024,12,64]{1,3,2,0:T(8,128)(2,1)} fusion(f32[2,12,256]{2,1,0:T(8,128)S(1)} %copy-done.42, f32[2,12,256,1024]{3,2,1,0:T(8,128)} %get-tuple-element.735, pred[2,1024]{1,0:T(4,128)(4,1)S(1)} %iota_compare_fusion.2, bf16[2,256,12,64]{1,0,3,2:T(2,128)(2,1)} %reshape.524), kind=kOutput, calls=%fused_computation.29.clone.1 | convolution fusion | flops 832045056 | bytes 29124608 | tf_op jit(solution)/shard_map/while/body/eval_jaxpr/shqk,sqhd->skhd/dot_general | solution.py:240
  277.7 5.3 select_add_fusion.8
  283.0 9.7 multiply_bitcast_fusion.2
  295.1 31.9 %reduce-scatter.20.cloned.1.call-done = bf16[2,256,12,64]{1,3,2,0:T(8,128)(2,1)} async-done(((bf16[2,1024,12,64]{1,3,2,0:T(8,128)(2,1)}), bf16[2,256,12,64]{1,3,2,0:T(8,128)(2,1)}) %reduce-scatter.20.cloned.1.call-update) | async-done | bytes 786448 | tf_op jit(solution)/shard_map/while/body/eval_jaxpr/reduce_scatter | solution.py:247
  338.3 4.3 select_add_fusion.6
  346.6 5.3 all-gather.10
  354.1 25.4 %all-gather.18.cloned.1.call-done = bf16[768,2304]{1,0:T(8,128)(2,1)} async-done(((bf16[192,2304]{1,0:T(8,128)(2,1)}), bf16[768,2304]{1,0:T(8,128)(2,1)}) %all-gather.18.cloned.1.call-update) | async-done | bytes 3538960 | tf_op jit(solution)/shard_map/while/body/eval_jaxpr/all_gather | solution.py:144
  379.5 5.7 copy.99
  400.7 32.7 %collective-permute-done.1 = bf16[2,256,12,64]{1,3,2,0:T(8,128)(2,1)S(1)} collective-permute-done((bf16[2,256,12,64]{1,3,2,0:T(8,128)(2,1)}, bf16[2,256,12,64]{1,3,2,0:T(8,128)(2,1)S(1)}, u32[]{:S(2)}, u32[]{:S(2)}) %collective-permute-start.1) | collective-permute-done | bytes 786464 | tf_op jit(solution)/shard_map/while/body/eval_jaxpr/ppermute | solution.py:39
  437.0 7.8 collective-permute-done.2
  450.9 10.3 fusion.188
  461.2 12.0 %fusion.189 = f32[2,12,256]{2,1,0:T(8,128)S(1)} fusion(f32[2,12,256]{2,1,0:T(8,128)S(1)} %get-tuple-element.734, f32[2,12,256,1024]{3,2,1,0:T(8,128)} %get-tuple-element.735, pred[2,1024]{1,0:T(4,128)(4,1)S(1)} %iota_compare_fusion.2), kind=kLoop, calls=%fused_computation.12.clone.1 | loop fusion | flops 25159680 | bytes 25217024 | tf_op jit(solution)/shard_map/while/body/eval_jaxpr/reduce_sum | solution.py:169
  474.5 12.6 %fusion.190 = bf16[2,256,12,64]{1,3,2,0:T(8,128)(2,1)S(1)} fusion(f32[2,12,256]{2,1,0:T(8,128)} %copy-done.48, f32[2,12,256]{2,1,0:T(8,128)} %copy-done.41, f32[2,12,256,1024]{3,2,1,0:T(8,128)} %get-tuple-element.735, pred[2,1024]{1,0:T(4,128)(4,1)S(1)} %iota_compare_fusion.2, bf16[2,1024,1,12,64]{1,4,3,2,0:T(8,128)(2,1)} %all-gather.20.cloned.1.call-done), kind=kOutput, calls=%fused_computation.71.clone.1 | convolution fusion | flops 837156864 | bytes 29149184 | tf_op jit(solution)/shard_map/while/body/eval_jaxpr/shqk,skhd->sqhd/dot_general | solution.py:172
  494.2 6.8 fusion.193
  501.0 11.2 %all-gather.26.cloned.1.call-done = bf16[1152,768]{1,0:T(8,128)(2,1)} async-done(((bf16[288,768]{1,0:T(8,128)(2,1)}), bf16[1152,768]{1,0:T(8,128)(2,1)}) %all-gather.26.cloned.1.call-update) | async-done | bytes 1769488 | tf_op jit(solution)/shard_map/while/body/eval_jaxpr/all_gather | solution.py:192
  512.3 6.4 fusion.196
  531.5 19.7 %multiply_reduce_fusion.9 = (f32[2,12,256]{2,1,0:T(8,128)}, f32[2,12,256,1024]{3,2,1,0:T(8,128)}) fusion(f32[2,12,256]{2,1,0:T(8,128)} %log_add_fusion.2, f32[2,12,256,1024]{3,2,1,0:T(8,128)} %get-tuple-element.735, pred[2,1024]{1,0:T(4,128)(4,1)S(1)} %iota_compare_fusion.2, bf16[2,1024,1,12,64]{1,4,3,2,0:T(8,128)(2,1)} %all-gather.20.cloned.1.call-done, ...), kind=kOutput, calls=%fused_computation.7.clone.1 | convolution fusion | flops 836757504 | bytes 54315008 | tf_op jit(solution)/shard_map/while/body/eval_jaxpr/sqhd,skhd->shqk/dot_general | solution.py:227
  551.3 16.9 %multiply_convert_fusion.13 = bf16[2,12,256,1024]{3,2,1,0:T(8,128)(2,1)S(1)} fusion(f32[2,12,256,1024]{3,2,1,0:T(8,128)} %get-tuple-element.747, f32[2,12,256]{2,1,0:T(8,128)} %get-tuple-element.748, f32[2,12,256]{2,1,0:T(8,128)} %log_add_fusion.2, f32[2,12,256,1024]{3,2,1,0:T(8,128)} %get-tuple-element.735, pred[2,1024]{1,0:T(4,128)(4,1)S(1)} %iota_compare_fusion.2), kind=kLoop, calls=%fused_computation.6.clone.1 | loop fusion | flops 37748736 | bytes 62965760 | tf_op jit(solution)/shard_map/while/body/eval_jaxpr/convert_element_type | solution.py:231
  568.2 4.6 copy-done
  577.5 14.3 %convert_bitcast_fusion.2 = bf16[2,1024,12,64]{1,3,2,0:T(8,128)(2,1)} fusion(f32[2,12,256]{2,1,0:T(8,128)S(1)} %copy-done.42, f32[2,12,256,1024]{3,2,1,0:T(8,128)} %get-tuple-element.735, pred[2,1024]{1,0:T(4,128)(4,1)S(1)} %iota_compare_fusion.2, bf16[2,256,12,64]{1,0,3,2:T(2,128)(2,1)} %reshape.524), kind=kOutput, calls=%fused_computation.29.clone.1 | convolution fusion | flops 832045056 | bytes 29124608 | tf_op jit(solution)/shard_map/while/body/eval_jaxpr/shqk,sqhd->skhd/dot_general | solution.py:240
  602.2 5.1 convolution_add_fusion.2
  607.4 8.3 select_add_fusion.8
  615.7 9.6 multiply_bitcast_fusion.2
  627.9 27.5 %reduce-scatter.20.cloned.1.call-done = bf16[2,256,12,64]{1,3,2,0:T(8,128)(2,1)} async-done(((bf16[2,1024,12,64]{1,3,2,0:T(8,128)(2,1)}), bf16[2,256,12,64]{1,3,2,0:T(8,128)(2,1)}) %reduce-scatter.20.cloned.1.call-update) | async-done | bytes 786448 | tf_op jit(solution)/shard_map/while/body/eval_jaxpr/reduce_scatter | solution.py:247
  686.9 5.2 convert_element_type.278
  692.2 5.1 convert_element_type.282
  697.4 4.7 reduce-scatter.18.cloned.1.call-done
  703.0 27.8 %reduce-scatter.12.cloned.1.call-done = bf16[192,768]{1,0:T(8,128)(2,1)} async-done(((bf16[768,768]{1,0:T(8,128)(2,1)}), bf16[192,768]{1,0:T(8,128)(2,1)}) %reduce-scatter.12.cloned.1.call-update) | async-done | bytes 294928 | tf_op jit(solution)/shard_map/reduce_scatter | solution.py:281
  730.8 32.5 %reduce-scatter.16.cloned.1.call-done = bf16[288,768]{1,0:T(8,128)(2,1)} async-done(((bf16[1152,768]{1,0:T(8,128)(2,1)}), bf16[288,768]{1,0:T(8,128)(2,1)}) %reduce-scatter.16.cloned.1.call-update) | async-done | bytes 442384 | tf_op jit(solution)/shard_map/reduce_scatter | solution.py:287
  763.3 42.9 %reduce-scatter.10.cloned.1.call-done = bf16[192,2304]{1,0:T(8,128)(2,1)} async-done(((bf16[768,2304]{1,0:T(8,128)(2,1)}), bf16[192,2304]{1,0:T(8,128)(2,1)}) %reduce-scatter.10.cloned.1.call-update) | async-done | bytes 884752 | tf_op jit(solution)/shard_map/reduce_scatter | solution.py:278
  806.3 43.1 %reduce-scatter.14.cloned.1.call-done = bf16[192,2304]{1,0:T(8,128)(2,1)} async-done(((bf16[768,2304]{1,0:T(8,128)(2,1)}), bf16[192,2304]{1,0:T(8,128)(2,1)}) %reduce-scatter.14.cloned.1.call-update) | async-done | bytes 884752 | tf_op jit(solution)/shard_map/reduce_scatter | solution.py:284
  849.3 199.6 %all-reduce.4 = (f32[192,2304]{1,0:T(8,128)}, f32[192,768]{1,0:T(8,128)}, f32[192,2304]{1,0:T(8,128)}, f32[288,768]{1,0:T(8,128)}, f32[2,192]{1,0:T(2,128)S(1)}) all-reduce(bf16[192,2304]{1,0:T(8,128)(2,1)} %reduce-scatter.10.cloned.1.call-done, ...), channel_id=1, replica_groups=mesh['dp'=8,'fsdp'=4] {'dp'}, use_global_device_ids=true, to_apply=%region_18.19 | all-reduce | flops 1253760 | bytes 7522560 | tf_op jit(solution)/shard_map/psum | solution.py:294
  1056.3 6.5 multiply_subtract_fusion.2
  (512 shorter events, 192.2 us)
Async XLA Ops:
  14.6 50.9 %copy-start.67 = (f32[256]{0:T(256)}, f32[256]{0:T(256)S(1)}, u32[]{:S(2)}) copy-start(f32[256]{0:T(256)S(1)} %get-tuple-element.826) | copy-start | bytes 3076 | tf_op jit(solution)/shard_map/while
  14.6 51.0 %copy-start.70 = (f32[32]{0:T(128)}, f32[32]{0:T(128)S(1)}, u32[]{:S(2)}) copy-start(f32[32]{0:T(128)S(1)} %get-tuple-element.825) | copy-start | bytes 388 | tf_op jit(solution)/shard_map/while
  14.6 36.5 %all-gather.18.cloned.1.call-start = ((), (), s32[]{:S(2)}) async-start(), calls=%async_computation.12 | async-start | bytes 4423680 | tf_op jit(solution)/shard_map/while/body/eval_jaxpr/all_gather | solution.py:144
  15.5 130.6 %all-gather.20.cloned.1.call-start = ((), (), s32[]{:S(2)}) async-start(), calls=%async_computation.13 | async-start | bytes 3932160 | tf_op jit(solution)/shard_map/while/body/eval_jaxpr/all_gather | solution.py:164
  22.1 34.7 %copy-start.54 = (f32[768]{0:T(1024)}, f32[768]{0:T(1024)S(1)}, u32[]{:S(2)}) copy-start(f32[768]{0:T(1024)S(1)} %get-tuple-element.723) | copy-start | bytes 9220 | tf_op jit(solution)/shard_map/while
  24.0 32.8 %copy-start.13 = (bf16[1,2,256,768]{3,2,1,0:T(8,128)(2,1)}, bf16[1,2,256,768]{3,2,1,0:T(8,128)(2,1)S(1)}, u32[]{:S(2)}) copy-start(bf16[1,2,256,768]{3,2,1,0:T(8,128)(2,1)S(1)} %fusion.184) | copy-start | bytes 2359300 | tf_op jit(solution)/shard_map/while
  64.2 96.6 %all-gather.22.cloned.1.call-start = ((), (), s32[]{:S(2)}) async-start(), calls=%async_computation.14 | async-start | bytes 1474560 | tf_op jit(solution)/shard_map/while/body/eval_jaxpr/all_gather | solution.py:145
  64.9 101.1 %all-gather.24.cloned.1.call-start = ((), (), s32[]{:S(2)}) async-start(), calls=%async_computation.15 | async-start | bytes 4423680 | tf_op jit(solution)/shard_map/while/body/eval_jaxpr/all_gather | solution.py:146
  65.5 118.4 %all-gather.26.cloned.1.call-start = ((), (), s32[]{:S(2)}) async-start(), calls=%async_computation.16 | async-start | bytes 2211840 | tf_op jit(solution)/shard_map/while/body/eval_jaxpr/all_gather | solution.py:192
  69.3 38.0 %copy-start.17 = (bf16[2,256,12,32]{1,3,2,0:T(8,128)(2,1)}, bf16[2,256,12,32]{1,3,2,0:T(8,128)(2,1)S(1)}, u32[]{:S(2)}) copy-start(bf16[2,256,12,32]{1,3,2,0:T(8,128)(2,1)S(1)} %get-tuple-element.730) | copy-start | bytes 1179652 | tf_op jit(solution)/shard_map/while
  69.3 38.0 %copy-start.19 = (bf16[2,256,12,32]{1,3,2,0:T(8,128)(2,1)}, bf16[2,256,12,32]{1,3,2,0:T(8,128)(2,1)S(1)}, u32[]{:S(2)}) copy-start(bf16[2,256,12,32]{1,3,2,0:T(8,128)(2,1)S(1)} %get-tuple-element.731) | copy-start | bytes 1179652 | tf_op jit(solution)/shard_map/while
  70.4 34.6 %collective-permute-start.1 = (bf16[2,256,12,64]{1,3,2,0:T(8,128)(2,1)}, bf16[2,256,12,64]{1,3,2,0:T(8,128)(2,1)S(1)}, u32[]{:S(2)}, u32[]{:S(2)}) collective-permute-start(bf16[2,256,12,64]{1,3,2,0:T(8,128)(2,1)} %pad_maximum_fusion.9), channel_id=1, source_target_pairs={{0,1},{1,2},{2,3},{3,0},{4,5},{5,6},{6,7},{7,4},{8,9},{9,10},{10,1... | collective-permute-start | bytes 2359304 | tf_op jit(solution)/shard_map/while/body/eval_jaxpr/ppermute | solution.py:39
  70.6 222.1 %reduce-scatter.22.cloned.1.call-start = ((), (), s32[]{:S(2)}) async-start(), calls=%async_computation.18 | async-start | bytes 3932160 | tf_op jit(solution)/shard_map/while/body/eval_jaxpr/reduce_scatter | solution.py:244
  70.8 37.8 %collective-permute-start = (bf16[2,256,12,64]{1,3,2,0:T(8,128)(2,1)}, bf16[2,256,12,64]{1,3,2,0:T(8,128)(2,1)S(1)}, u32[]{:S(2)}, u32[]{:S(2)}) collective-permute-start(bf16[2,256,12,64]{1,3,2,0:T(8,128)(2,1)} %pad_maximum_fusion.9), channel_id=1, source_target_pairs={{1,0},{2,1},{3,2},{0,3},{5,4},{6,5},{7,6},{4,7},{9,8},{10,9},{11,1... | collective-permute-start | bytes 2359304 | tf_op jit(solution)/shard_map/while/body/eval_jaxpr/ppermute | solution.py:42
  104.9 11.4 %collective-permute-start.2 = (bf16[2,256,12,64]{1,3,2,0:T(8,128)(2,1)S(1)}, bf16[2,256,12,64]{1,3,2,0:T(8,128)(2,1)S(1)}, u32[]{:S(2)}, u32[]{:S(2)}) collective-permute-start(bf16[2,256,12,64]{1,3,2,0:T(8,128)(2,1)S(1)} %collective-permute-done.1), channel_id=1, source_target_pairs={{0,1},{1,2},{2,3},{3,0},{4,5},{5,6},{6,7},{7,4},{8,9},{9,10},{10,1... | collective-permute-start | bytes 2359304 | tf_op jit(solution)/shard_map/while/body/eval_jaxpr/ppermute | solution.py:39
  132.8 12.0 %copy-start.41 = (f32[2,12,256]{2,1,0:T(8,128)}, f32[2,12,256]{2,1,0:T(8,128)S(1)}, u32[]{:S(2)}) copy-start(f32[2,12,256]{2,1,0:T(8,128)S(1)} %get-tuple-element.734) | copy-start | bytes 73732 | tf_op jit(solution)/shard_map/while
  222.6 21.5 %copy-start.16 = (bf16[2,256,12,32]{1,3,2,0:T(8,128)(2,1)S(1)}, bf16[2,256,12,32]{1,3,2,0:T(8,128)(2,1)}, u32[]{:S(2)}) copy-start(bf16[2,256,12,32]{1,3,2,0:T(8,128)(2,1)} %get-tuple-element.732) | copy-start | bytes 1179652 | tf_op jit(solution)/shard_map/while
  248.1 78.8 %reduce-scatter.20.cloned.1.call-start = ((), (), s32[]{:S(2)}) async-start(), calls=%async_computation.17 | async-start | bytes 3932160 | tf_op jit(solution)/shard_map/while/body/eval_jaxpr/reduce_scatter | solution.py:247
  328.3 9.8 slice-start
  345.6 48.3 %copy-start.67 = (f32[256]{0:T(256)}, f32[256]{0:T(256)S(1)}, u32[]{:S(2)}) copy-start(f32[256]{0:T(256)S(1)} %get-tuple-element.826) | copy-start | bytes 3076 | tf_op jit(solution)/shard_map/while
  345.6 48.3 %copy-start.70 = (f32[32]{0:T(128)}, f32[32]{0:T(128)S(1)}, u32[]{:S(2)}) copy-start(f32[32]{0:T(128)S(1)} %get-tuple-element.825) | copy-start | bytes 388 | tf_op jit(solution)/shard_map/while
  345.7 33.8 %all-gather.18.cloned.1.call-start = ((), (), s32[]{:S(2)}) async-start(), calls=%async_computation.12 | async-start | bytes 4423680 | tf_op jit(solution)/shard_map/while/body/eval_jaxpr/all_gather | solution.py:144
  346.6 128.0 %all-gather.20.cloned.1.call-start = ((), (), s32[]{:S(2)}) async-start(), calls=%async_computation.13 | async-start | bytes 3932160 | tf_op jit(solution)/shard_map/while/body/eval_jaxpr/all_gather | solution.py:164
  352.2 33.0 %copy-start.54 = (f32[768]{0:T(1024)}, f32[768]{0:T(1024)S(1)}, u32[]{:S(2)}) copy-start(f32[768]{0:T(1024)S(1)} %get-tuple-element.723) | copy-start | bytes 9220 | tf_op jit(solution)/shard_map/while
  354.0 31.2 %copy-start.13 = (bf16[1,2,256,768]{3,2,1,0:T(8,128)(2,1)}, bf16[1,2,256,768]{3,2,1,0:T(8,128)(2,1)S(1)}, u32[]{:S(2)}) copy-start(bf16[1,2,256,768]{3,2,1,0:T(8,128)(2,1)S(1)} %fusion.184) | copy-start | bytes 2359300 | tf_op jit(solution)/shard_map/while
  392.6 96.4 %all-gather.22.cloned.1.call-start = ((), (), s32[]{:S(2)}) async-start(), calls=%async_computation.14 | async-start | bytes 1474560 | tf_op jit(solution)/shard_map/while/body/eval_jaxpr/all_gather | solution.py:145
  393.1 101.1 %all-gather.24.cloned.1.call-start = ((), (), s32[]{:S(2)}) async-start(), calls=%async_computation.15 | async-start | bytes 4423680 | tf_op jit(solution)/shard_map/while/body/eval_jaxpr/all_gather | solution.py:146
  393.9 118.4 %all-gather.26.cloned.1.call-start = ((), (), s32[]{:S(2)}) async-start(), calls=%async_computation.16 | async-start | bytes 2211840 | tf_op jit(solution)/shard_map/while/body/eval_jaxpr/all_gather | solution.py:192
  397.7 38.0 %copy-start.17 = (bf16[2,256,12,32]{1,3,2,0:T(8,128)(2,1)}, bf16[2,256,12,32]{1,3,2,0:T(8,128)(2,1)S(1)}, u32[]{:S(2)}) copy-start(bf16[2,256,12,32]{1,3,2,0:T(8,128)(2,1)S(1)} %get-tuple-element.730) | copy-start | bytes 1179652 | tf_op jit(solution)/shard_map/while
  397.7 38.0 %copy-start.19 = (bf16[2,256,12,32]{1,3,2,0:T(8,128)(2,1)}, bf16[2,256,12,32]{1,3,2,0:T(8,128)(2,1)S(1)}, u32[]{:S(2)}) copy-start(bf16[2,256,12,32]{1,3,2,0:T(8,128)(2,1)S(1)} %get-tuple-element.731) | copy-start | bytes 1179652 | tf_op jit(solution)/shard_map/while
  398.8 34.6 %collective-permute-start.1 = (bf16[2,256,12,64]{1,3,2,0:T(8,128)(2,1)}, bf16[2,256,12,64]{1,3,2,0:T(8,128)(2,1)S(1)}, u32[]{:S(2)}, u32[]{:S(2)}) collective-permute-start(bf16[2,256,12,64]{1,3,2,0:T(8,128)(2,1)} %pad_maximum_fusion.9), channel_id=1, source_target_pairs={{0,1},{1,2},{2,3},{3,0},{4,5},{5,6},{6,7},{7,4},{8,9},{9,10},{10,1... | collective-permute-start | bytes 2359304 | tf_op jit(solution)/shard_map/while/body/eval_jaxpr/ppermute | solution.py:39
  399.0 226.3 %reduce-scatter.22.cloned.1.call-start = ((), (), s32[]{:S(2)}) async-start(), calls=%async_computation.18 | async-start | bytes 3932160 | tf_op jit(solution)/shard_map/while/body/eval_jaxpr/reduce_scatter | solution.py:244
  399.2 37.8 %collective-permute-start = (bf16[2,256,12,64]{1,3,2,0:T(8,128)(2,1)}, bf16[2,256,12,64]{1,3,2,0:T(8,128)(2,1)S(1)}, u32[]{:S(2)}, u32[]{:S(2)}) collective-permute-start(bf16[2,256,12,64]{1,3,2,0:T(8,128)(2,1)} %pad_maximum_fusion.9), channel_id=1, source_target_pairs={{1,0},{2,1},{3,2},{0,3},{5,4},{6,5},{7,6},{4,7},{9,8},{10,9},{11,1... | collective-permute-start | bytes 2359304 | tf_op jit(solution)/shard_map/while/body/eval_jaxpr/ppermute | solution.py:42
  433.4 11.4 %collective-permute-start.2 = (bf16[2,256,12,64]{1,3,2,0:T(8,128)(2,1)S(1)}, bf16[2,256,12,64]{1,3,2,0:T(8,128)(2,1)S(1)}, u32[]{:S(2)}, u32[]{:S(2)}) collective-permute-start(bf16[2,256,12,64]{1,3,2,0:T(8,128)(2,1)S(1)} %collective-permute-done.1), channel_id=1, source_target_pairs={{0,1},{1,2},{2,3},{3,0},{4,5},{5,6},{6,7},{7,4},{8,9},{9,10},{10,1... | collective-permute-start | bytes 2359304 | tf_op jit(solution)/shard_map/while/body/eval_jaxpr/ppermute | solution.py:39
  461.2 12.0 %copy-start.41 = (f32[2,12,256]{2,1,0:T(8,128)}, f32[2,12,256]{2,1,0:T(8,128)S(1)}, u32[]{:S(2)}) copy-start(f32[2,12,256]{2,1,0:T(8,128)S(1)} %get-tuple-element.734) | copy-start | bytes 73732 | tf_op jit(solution)/shard_map/while
  551.3 21.5 %copy-start.16 = (bf16[2,256,12,32]{1,3,2,0:T(8,128)(2,1)S(1)}, bf16[2,256,12,32]{1,3,2,0:T(8,128)(2,1)}, u32[]{:S(2)}) copy-start(bf16[2,256,12,32]{1,3,2,0:T(8,128)(2,1)} %get-tuple-element.732) | copy-start | bytes 1179652 | tf_op jit(solution)/shard_map/while
  576.8 78.7 %reduce-scatter.20.cloned.1.call-start = ((), (), s32[]{:S(2)}) async-start(), calls=%async_computation.17 | async-start | bytes 3932160 | tf_op jit(solution)/shard_map/while/body/eval_jaxpr/reduce_scatter | solution.py:247
  678.9 23.2 %reduce-scatter.18.cloned.1.call-start = ((), (), s32[]{:S(2)}) async-start(), calls=%async_computation.11 | async-start | bytes 245760
  680.6 50.3 %reduce-scatter.12.cloned.1.call-start = ((), (), s32[]{:S(2)}) async-start(), calls=%async_computation.8 | async-start | bytes 1474560 | tf_op jit(solution)/shard_map/reduce_scatter | solution.py:281
  683.4 79.9 %reduce-scatter.16.cloned.1.call-start = ((), (), s32[]{:S(2)}) async-start(), calls=%async_computation.10 | async-start | bytes 2211840 | tf_op jit(solution)/shard_map/reduce_scatter | solution.py:287
  686.9 119.4 %reduce-scatter.10.cloned.1.call-start = ((), (), s32[]{:S(2)}) async-start(), calls=%async_computation.7 | async-start | bytes 4423680 | tf_op jit(solution)/shard_map/reduce_scatter | solution.py:278
  692.2 157.1 %reduce-scatter.14.cloned.1.call-start = ((), (), s32[]{:S(2)}) async-start(), calls=%async_computation.9 | async-start | bytes 4423680 | tf_op jit(solution)/shard_map/reduce_scatter | solution.py:284
  697.4 355.3 %copy-start.56 = (f32[288,768]{1,0:T(8,128)S(1)}, f32[288,768]{1,0:T(8,128)}, u32[]{:S(2)}) copy-start(f32[288,768]{1,0:T(8,128)} %param.31) | copy-start | bytes 2654212
  697.4 351.6 %copy-start.72 = (f32[2,192]{1,0:T(2,128)S(1)}, f32[2,192]{1,0:T(2,128)}, u32[]{:S(2)}) copy-start(f32[2,192]{1,0:T(2,128)} %param.27) | copy-start | bytes 4612
  697.4 351.6 %copy-start.73 = (f32[2,192]{1,0:T(2,128)S(1)}, f32[2,192]{1,0:T(2,128)}, u32[]{:S(2)}) copy-start(f32[2,192]{1,0:T(2,128)} %param.32) | copy-start | bytes 4612
  697.4 351.6 %copy-start.74 = (f32[2,192]{1,0:T(2,128)S(1)}, f32[2,192]{1,0:T(2,128)}, u32[]{:S(2)}) copy-start(f32[2,192]{1,0:T(2,128)} %param.37) | copy-start | bytes 4612
  697.4 352.2 %copy-start.49 = (f32[192,768]{1,0:T(8,128)S(1)}, f32[192,768]{1,0:T(8,128)}, u32[]{:S(2)}) copy-start(f32[192,768]{1,0:T(8,128)} %param.24) | copy-start | bytes 1769476
  849.3 207.0 %copy-start.53 = (f32[192,2304]{1,0:T(8,128)S(1)}, f32[192,2304]{1,0:T(8,128)}, u32[]{:S(2)}) copy-start(f32[192,2304]{1,0:T(8,128)} %param.28) | copy-start | bytes 5308420
  (130 other events, 444.3 us)
Sparse Core Ops, SparseCore 0:
  17.6 33.4 all-gather.17
  64.3 44.9 all-gather.19
  110.9 17.3 all-gather.21
  130.3 30.7 all-gather.23
  163.1 20.7 all-gather.25
  248.2 37.9 reduce-scatter.21
  288.9 37.9 reduce-scatter.19
  348.6 30.7 all-gather.17
  392.7 44.9 all-gather.19
  439.1 17.4 all-gather.21
  458.7 30.7 all-gather.23
  491.5 20.7 all-gather.25
  576.9 37.9 reduce-scatter.21
  617.4 37.9 reduce-scatter.19
Sparse Core Ops, SparseCore 1:
  682.4 19.7 reduce-scatter.17
  705.2 25.6 reduce-scatter.11
  734.0 29.2 reduce-scatter.15
  765.9 40.3 reduce-scatter.9
  809.0 40.2 reduce-scatter.13
